TPU v7x, 32 devices: a whole 2x2x4 slice. The times are simulated.
32 devices in a mesh: aux: 8 (over y, x, core), shell: 4 (over z).
Axes of the slice: x: 2, y: 2, z: 4, core: 2. Of those that a mesh axis runs over, the one named last changes fastest.
Arguments:
- density: bfloat16 [32, 120, 8192], P('aux', None, 'shell'), may hold values from -6 to 6
- occ_density: bfloat16 [32, 120, 120], P('aux'), may hold values from -6 to 6
- cabs_coeff: bfloat16 [2048, 8192], P('aux', 'shell'), may hold values from -0.0625 to 0.0625
- occ_coeff: bfloat16 [2048, 120], P('aux'), may hold values from -0.5 to 0.5
- tile_owner: int32 [16, 1], replicated, may hold values from 0 to 3; in each aligned block of 16 rows (0 to 15, 16 to 31, ...) at most 8 rows name the same one
Outputs:
- ao_density: bfloat16 [32, 32, 128, 2048], P('shell', 'aux')
Inputs may be any that keep to these rules, and one draw needn't show every extreme that they name: `tile_owner`: no owner holds more than 8 blocks, and some owner holds exactly 8; every owner holds at least one block.
All inputs are finite; a program needn't handle non-finite values.
Results may differ from a plain program's by a relative error of at most 0.015.
Values may be sent and summed in bfloat16 or wider, within the bound.
No kernel may reach another device: no remote copies, remote signals or barrier semaphores. Data moves between devices by JAX's collectives and lax.ppermute only.
A program may use at most 64 MiB of HBM per device.

v0:
```python
import jax
import jax.numpy as jnp
from jax import lax
from jax.sharding import PartitionSpec as P

NOCC = 120
CAPT = 8


def per_device(density, occ_density, cabs_coeff, occ_coeff, tile_owner):
    local_q = density.shape[0]
    owners = lax.axis_size("shell")
    me_shell = lax.axis_index("shell")
    occ_full = lax.all_gather(occ_coeff, "aux", axis=0, tiled=True)
    nao = occ_full.shape[0]
    ntile = tile_owner.shape[0]
    width = nao // ntile
    share_cols = nao // owners
    owned = (tile_owner[:, 0] == me_shell).astype(jnp.int32)
    rank = jnp.cumsum(owned) - 1
    select = (
        (rank[None, :] == jnp.arange(CAPT, dtype=jnp.int32)[:, None]) & (owned[None, :] == 1)
    ).astype(jnp.bfloat16)
    batches = 2
    span = local_q // batches
    results = []
    for batch in range(batches):
        dens = density[batch * span : (batch + 1) * span]
        occ_dens = occ_density[batch * span : (batch + 1) * span]
        flat = dens.reshape(span * NOCC, dens.shape[2])
        terms = lax.dot_general(
            flat,
            lax.all_gather(cabs_coeff, "aux", axis=0, tiled=True),
            (((1,), (1,)), ((), ())),
            preferred_element_type=jnp.float32,
        )
        mine = lax.psum_scatter(
            terms.astype(jnp.bfloat16), "shell", scatter_dimension=1, tiled=True
        ).astype(jnp.float32)
        my_rows = lax.dynamic_slice_in_dim(occ_full, me_shell * share_cols, share_cols, 0)
        occ_term = jnp.einsum("qij,nj->qin", occ_dens, my_rows, preferred_element_type=jnp.float32)
        rounded = (mine + occ_term.reshape(span * NOCC, share_cols)).astype(jnp.bfloat16)
        spread = lax.all_gather(rounded, "shell", axis=1, tiled=True)
        blocks = spread.reshape(span, NOCC, ntile, width)
        half_owned = jnp.einsum(
            "kt,qitw->kqiw", select, blocks, preferred_element_type=jnp.float32
        ).astype(jnp.bfloat16)
        gamma = jnp.einsum(
            "kqiw,mi->kqwm", half_owned, occ_full, preferred_element_type=jnp.float32
        )
        results.append(gamma.astype(jnp.bfloat16))
    return jnp.concatenate(results, axis=1)


def solution(mesh):
    in_specs = (
        P("aux", None, "shell"),
        P("aux", None, None),
        P("aux", "shell"),
        P("aux", None),
        P(),
    )
    out_specs = P("shell", "aux", None, None)
    return jax.shard_map(
        per_device, mesh=mesh, in_specs=in_specs, out_specs=out_specs, check_vma=False
    )
```

profile of v0, /device:TPU:0, one launch (start us, length us, event | category | flops | bytes accessed | tf_op | source)
XLA Modules:
  0.0 177.0 jit_solution(4344469540848584070)
XLA Ops:
  6.5 0.7 all-gather.2.cloned.1.call-update
  7.3 1.6 fusion.26
  8.9 57.3 %all-gather.2.cloned.1.call-done = bf16[2048,2048]{1,0:T(8,128)(2,1)} async-done(((bf16[256,2048]{1,0:T(8,128)(2,1)}), bf16[2048,2048]{1,0:T(8,128)(2,1)}) %all-gather.2.cloned.1.call-update) | async-done | bytes 8388624 | tf_op jit(solution)/shard_map/all_gather | solution.py:33
  66.2 6.8 %convolution_convert_fusion.3 = bf16[240,2048]{1,0:T(8,128)(2,1)} fusion(bf16[240,2048]{1,0:T(8,128)(2,1)S(1)} %bitcast.57, bf16[2048,2048]{1,0:T(8,128)(2,1)} %all-gather.2.cloned.1.call-done), kind=kOutput, calls=%fused_computation.4 | convolution fusion | flops 2013757440 | bytes 10354688 | tf_op jit(solution)/shard_map/dot_general | solution.py:31
  73.0 0.0 reduce-scatter.5.cloned.1.call-start
  73.1 6.7 %convolution_convert_fusion.2 = bf16[240,2048]{1,0:T(8,128)(2,1)} fusion(bf16[240,2048]{1,0:T(8,128)(2,1)S(1)} %bitcast.56, bf16[2048,2048]{1,0:T(8,128)(2,1)} %all-gather.2.cloned.1.call-done), kind=kOutput, calls=%fused_computation.3 | convolution fusion | flops 2013757440 | bytes 10354688 | tf_op jit(solution)/shard_map/dot_general | solution.py:31
  79.9 0.1 copy.7
  80.0 10.9 %all_gather.14 = bf16[2048,120]{0,1:T(8,128)(2,1)S(1)} all-gather(bf16[256,120]{0,1:T(8,128)(2,1)S(1)} %copy-done.1), channel_id=1, replica_groups=mesh['aux'=8,'shell'=4] {'aux'}, dimensions={0}, use_global_device_ids=true | all-gather | bytes 552960 | tf_op jit(solution)/shard_map/all_gather | solution.py:14
  90.8 0.1 add_reduce_fusion
  91.0 0.2 fusion.8
  91.2 0.2 fusion.10
  91.4 8.0 %reduce-scatter.3.cloned.1.call-done = bf16[240,512]{1,0:T(8,128)(2,1)} async-done(((bf16[240,2048]{1,0:T(8,128)(2,1)}), bf16[240,512]{1,0:T(8,128)(2,1)}) %reduce-scatter.3.cloned.1.call-update) | async-done | bytes 245776 | tf_op jit(solution)/shard_map/reduce_scatter | solution.py:37
  99.5 1.0 fusion.5
  100.5 31.1 %all_gather.15 = bf16[240,2048]{1,0:T(8,128)(2,1)S(1)} all-gather(bf16[240,512]{1,0:T(8,128)(2,1)S(1)} %fusion.5), channel_id=1, replica_groups=mesh['aux'=8,'shell'=4] {'shell'}, dimensions={1}, use_global_device_ids=true | all-gather | bytes 1228800 | tf_op jit(solution)/shard_map/all_gather | solution.py:43
  131.5 0.2 copy.12
  131.8 4.9 %reduce-scatter.5.cloned.1.call-done = bf16[240,512]{1,0:T(8,128)(2,1)} async-done(((bf16[240,2048]{1,0:T(8,128)(2,1)}), bf16[240,512]{1,0:T(8,128)(2,1)}) %reduce-scatter.5.cloned.1.call-update) | async-done | bytes 245776 | tf_op jit(solution)/shard_map/reduce_scatter | solution.py:37
  136.7 1.0 fusion.4
  137.7 20.5 %all_gather.16 = bf16[240,2048]{1,0:T(8,128)(2,1)S(1)} all-gather(bf16[240,512]{1,0:T(8,128)(2,1)S(1)} %fusion.4), channel_id=1, replica_groups=mesh['aux'=8,'shell'=4] {'shell'}, dimensions={1}, use_global_device_ids=true | all-gather | bytes 1228800 | tf_op jit(solution)/shard_map/all_gather | solution.py:43
  158.2 0.2 copy.13
  158.4 0.3 fusion.2
  158.7 0.3 fusion
  159.0 2.4 %convolution_convert_fusion = bf16[8,2,128,2048]{3,2,1,0:T(8,128)(2,1)S(1)} fusion(bf16[8,2,120,128]{3,0,2,1:T(8,128)(2,1)S(1)} %fusion, bf16[2048,120]{0,1:T(8,128)(2,1)S(1)} %all_gather.14), kind=kOutput, calls=%fused_computation.1 | convolution fusion | flops 1010827264 | bytes 9371648 | tf_op jit(solution)/shard_map/kqiw,mi->kqwm/dot_general | solution.py:48
  161.4 2.4 %convolution_convert_fusion.1 = bf16[8,2,128,2048]{3,2,1,0:T(8,128)(2,1)S(1)} fusion(bf16[8,2,120,128]{3,0,2,1:T(8,128)(2,1)S(1)} %fusion.2, bf16[2048,120]{0,1:T(8,128)(2,1)S(1)} %all_gather.14), kind=kOutput, calls=%fused_computation.2 | convolution fusion | flops 1010827264 | bytes 9371648 | tf_op jit(solution)/shard_map/kqiw,mi->kqwm/dot_general | solution.py:48
  163.8 6.7 %pad_maximum_fusion = bf16[8,4,128,2048]{3,2,1,0:T(8,128)(2,1)} fusion(bf16[8,2,128,2048]{3,2,1,0:T(8,128)(2,1)S(1)} %convolution_convert_fusion, bf16[8,2,128,2048]{3,2,1,0:T(8,128)(2,1)S(1)} %convolution_convert_fusion.1), kind=kLoop, calls=%fused_computation | loop fusion | flops 8388608 | bytes 33554432 | tf_op jit(solution)/shard_map/concatenate | solution.py:52
  (12 shorter events, 0.1 us)
Async XLA Ops:
  6.5 59.7 %all-gather.2.cloned.1.call-start = ((), (), s32[]{:S(2)}) async-start(), calls=%async_computation.2 | async-start | bytes 9437184 | tf_op jit(solution)/shard_map/all_gather | solution.py:33
  7.3 92.2 %reduce-scatter.3.cloned.1.call-start = ((), (), s32[]{:S(2)}) async-start(), calls=%async_computation.3 | async-start | bytes 1228800 | tf_op jit(solution)/shard_map/reduce_scatter | solution.py:37
  73.0 6.8 %copy-start.2 = (s32[16,1]{0,1:T(1,128)S(1)}, s32[16,1]{0,1:T(1,128)}, u32[]{:S(2)}) copy-start(s32[16,1]{0,1:T(1,128)} %param.9) | copy-start | bytes 196
  73.0 7.0 %copy-start.1 = (bf16[256,120]{0,1:T(8,128)(2,1)S(1)}, bf16[256,120]{0,1:T(8,128)(2,1)}, u32[]{:S(2)}) copy-start(bf16[256,120]{0,1:T(8,128)(2,1)} %param.8) | copy-start | bytes 184324
  73.0 17.9 %copy-start = (bf16[4,120,120]{2,1,0:T(8,128)(2,1)S(1)}, bf16[4,120,120]{2,1,0:T(8,128)(2,1)}, u32[]{:S(2)}) copy-start(bf16[4,120,120]{2,1,0:T(8,128)(2,1)} %param.6) | copy-start | bytes 345604
  73.0 63.6 %reduce-scatter.5.cloned.1.call-start = ((), (), s32[]{:S(2)}) async-start(), calls=%async_computation.4 | async-start | bytes 1228800 | tf_op jit(solution)/shard_map/reduce_scatter | solution.py:37
Sparse Core Ops, SparseCore 0:
  9.2 56.9 all-gather.1
  73.2 26.2 reduce-scatter.2
  101.8 34.8 reduce-scatter.4
where the time goes:
time: 177 us
  waiting for transfers between devices  71 us (40%)
  blocking collectives  62.4 us (35%)
  matrix products  19.3 us (11%)
  between operations  13.2 us (7%)
  other arithmetic  8.89 us (5%)
  local copies, waits for them, and re-layouts  2.12 us (1%)
    all_gather x1, waiting for transfers between devices, per_device(): lax.all_gather(cabs_coeff, 'aux', axis=0, tiled=True)  57.3 us
    all_gather x2, blocking collectives, per_device(): spread = lax.all_gather(rounded, 'shell', axis=1, tiled=True)  51.6 us
    dot_general x2, matrix products, per_device(): lax.dot_general(flat, lax.all_gather(cabs_coeff, 'aux', axis=0, tiled=Tru...  13.5 us
    reduce_scatter x2, waiting for transfers between devices, per_device(): lax.psum_scatter(terms.astype(jnp.bfloat16), 'shell', scatter_dimension=1...  12.9 us
    all_gather x1, blocking collectives, per_device(): occ_full = lax.all_gather(occ_coeff, 'aux', axis=0, tiled=True)  10.9 us
    concatenate x1, other arithmetic, per_device(): return jnp.concatenate(results, axis=1)  6.71 us
    dot_general x2, matrix products, per_device(): jnp.einsum('kqiw,mi->kqwm', half_owned, occ_full, preferred_element_type=...  4.81 us
  transfers between devices with their start and end apart: 3, of which 3 were waited for; matrix products, arithmetic and copies ran while one was open for 6% of the time, Pallas kernels for 0%

commit v1 on v0

--- a/solution.py
+++ b/solution.py
@@ -40,7 +40,8 @@
         my_rows = lax.dynamic_slice_in_dim(occ_full, me_shell * share_cols, share_cols, 0)
         occ_term = jnp.einsum("qij,nj->qin", occ_dens, my_rows, preferred_element_type=jnp.float32)
         rounded = (mine + occ_term.reshape(span * NOCC, share_cols)).astype(jnp.bfloat16)
-        spread = lax.all_gather(rounded, "shell", axis=1, tiled=True)
+        shards = lax.all_gather(rounded, "shell", axis=0, tiled=False)
+        spread = jnp.concatenate(shards, axis=1)
         blocks = spread.reshape(span, NOCC, ntile, width)
         half_owned = jnp.einsum(
             "kt,qitw->kqiw", select, blocks, preferred_element_type=jnp.float32

time: 177 us -> 178 us (level)
  local copies, waits for them, and re-layouts: 2.12 us -> 3.99 us
where the time goes in v1:
time: 178 us
  waiting for transfers between devices  70.1 us (39%)
  blocking collectives  62.6 us (35%)
  matrix products  19.3 us (11%)
  between operations  13.2 us (7%)
  other arithmetic  8.89 us (5%)
  local copies, waits for them, and re-layouts  3.99 us (2%)
    all_gather x1, waiting for transfers between devices, per_device(): lax.all_gather(cabs_coeff, 'aux', axis=0, tiled=True)  57.3 us
    all_gather x2, blocking collectives, per_device(): shards = lax.all_gather(rounded, 'shell', axis=0, tiled=False)  51.8 us
    dot_general x2, matrix products, per_device(): lax.dot_general(flat, lax.all_gather(cabs_coeff, 'aux', axis=0, tiled=Tru...  13.5 us
    reduce_scatter x2, waiting for transfers between devices, per_device(): lax.psum_scatter(terms.astype(jnp.bfloat16), 'shell', scatter_dimension=1...  12 us
    all_gather x1, blocking collectives, per_device(): occ_full = lax.all_gather(occ_coeff, 'aux', axis=0, tiled=True)  10.9 us
    concatenate x1, other arithmetic, per_device(): return jnp.concatenate(results, axis=1)  6.71 us
    dot_general x2, matrix products, per_device(): jnp.einsum('kqiw,mi->kqwm', half_owned, occ_full, preferred_element_type=...  4.81 us
  transfers between devices with their start and end apart: 3, of which 3 were waited for; matrix products, arithmetic and copies ran while one was open for 6% of the time, Pallas kernels for 0%

profile of v1, /device:TPU:0, one launch (start us, length us, event | category | flops | bytes accessed | tf_op | source)
XLA Modules:
  0.0 178.1 jit_solution(10119550829804551322)
XLA Ops:
  6.5 0.7 all-gather.4.cloned.1.call-update
  7.3 1.6 fusion.24
  8.9 57.3 %all-gather.4.cloned.1.call-done = bf16[2048,2048]{1,0:T(8,128)(2,1)} async-done(((bf16[256,2048]{1,0:T(8,128)(2,1)}), bf16[2048,2048]{1,0:T(8,128)(2,1)}) %all-gather.4.cloned.1.call-update) | async-done | bytes 8388624 | tf_op jit(solution)/shard_map/all_gather | solution.py:33
  66.2 6.8 %convolution_convert_fusion.3 = bf16[240,2048]{1,0:T(8,128)(2,1)} fusion(bf16[240,2048]{1,0:T(8,128)(2,1)S(1)} %bitcast.53, bf16[2048,2048]{1,0:T(8,128)(2,1)} %all-gather.4.cloned.1.call-done), kind=kOutput, calls=%fused_computation.4 | convolution fusion | flops 2013757440 | bytes 10354688 | tf_op jit(solution)/shard_map/dot_general | solution.py:31
  73.1 6.7 %convolution_convert_fusion.2 = bf16[240,2048]{1,0:T(8,128)(2,1)} fusion(bf16[240,2048]{1,0:T(8,128)(2,1)S(1)} %bitcast.52, bf16[2048,2048]{1,0:T(8,128)(2,1)} %all-gather.4.cloned.1.call-done), kind=kOutput, calls=%fused_computation.3 | convolution fusion | flops 2013757440 | bytes 10354688 | tf_op jit(solution)/shard_map/dot_general | solution.py:31
  80.0 10.9 %all_gather.20 = bf16[2048,120]{0,1:T(8,128)(2,1)S(1)} all-gather(bf16[256,120]{0,1:T(8,128)(2,1)S(1)} %copy-done.1), channel_id=1, replica_groups=mesh['aux'=8,'shell'=4] {'aux'}, dimensions={0}, use_global_device_ids=true | all-gather | bytes 552960 | tf_op jit(solution)/shard_map/all_gather | solution.py:14
  90.8 0.1 add_reduce_fusion
  91.0 0.2 fusion.4
  91.2 0.2 fusion.6
  91.4 8.0 %reduce-scatter.3.cloned.1.call-done = bf16[240,512]{1,0:T(8,128)(2,1)} async-done(((bf16[240,2048]{1,0:T(8,128)(2,1)}), bf16[240,512]{1,0:T(8,128)(2,1)}) %reduce-scatter.3.cloned.1.call-update) | async-done | bytes 245776 | tf_op jit(solution)/shard_map/reduce_scatter | solution.py:37
  99.4 1.0 fusion.1
  100.5 31.1 %all-gather = bf16[960,512]{1,0:T(8,128)(2,1)S(1)} all-gather(bf16[240,512]{1,0:T(8,128)(2,1)S(1)} %fusion.1), channel_id=2, replica_groups=mesh['aux'=8,'shell'=4] {'shell'}, dimensions={0}, use_global_device_ids=true | all-gather | bytes 1228800 | tf_op jit(solution)/shard_map/all_gather | solution.py:43
  131.6 0.8 copy.21
  132.3 0.4 reshape_reshape.6
  132.7 4.0 %reduce-scatter.5.cloned.1.call-done = bf16[240,512]{1,0:T(8,128)(2,1)} async-done(((bf16[240,2048]{1,0:T(8,128)(2,1)}), bf16[240,512]{1,0:T(8,128)(2,1)}) %reduce-scatter.5.cloned.1.call-update) | async-done | bytes 245776 | tf_op jit(solution)/shard_map/reduce_scatter | solution.py:37
  136.7 1.0 fusion
  137.7 20.7 %all-gather.1 = bf16[960,512]{1,0:T(8,128)(2,1)S(1)} all-gather(bf16[240,512]{1,0:T(8,128)(2,1)S(1)} %fusion), channel_id=3, replica_groups=mesh['aux'=8,'shell'=4] {'shell'}, dimensions={0}, use_global_device_ids=true | all-gather | bytes 1228800 | tf_op jit(solution)/shard_map/all_gather | solution.py:43
  158.4 0.8 copy.20
  159.1 0.4 reshape_reshape.7
  159.5 0.3 fusion.16
  159.8 0.3 fusion.14
  160.1 2.4 %convolution_convert_fusion = bf16[8,2,128,2048]{3,2,1,0:T(8,128)(2,1)S(1)} fusion(bf16[8,2,120,128]{3,0,2,1:T(8,128)(2,1)S(1)} %fusion.14, bf16[2048,120]{0,1:T(8,128)(2,1)S(1)} %all_gather.20), kind=kOutput, calls=%fused_computation.1 | convolution fusion | flops 1010827264 | bytes 9371648 | tf_op jit(solution)/shard_map/kqiw,mi->kqwm/dot_general | solution.py:49
  162.5 2.4 %convolution_convert_fusion.1 = bf16[8,2,128,2048]{3,2,1,0:T(8,128)(2,1)S(1)} fusion(bf16[8,2,120,128]{3,0,2,1:T(8,128)(2,1)S(1)} %fusion.16, bf16[2048,120]{0,1:T(8,128)(2,1)S(1)} %all_gather.20), kind=kOutput, calls=%fused_computation.2 | convolution fusion | flops 1010827264 | bytes 9371648 | tf_op jit(solution)/shard_map/kqiw,mi->kqwm/dot_general | solution.py:49
  164.9 6.7 %pad_maximum_fusion = bf16[8,4,128,2048]{3,2,1,0:T(8,128)(2,1)} fusion(bf16[8,2,128,2048]{3,2,1,0:T(8,128)(2,1)S(1)} %convolution_convert_fusion, bf16[8,2,128,2048]{3,2,1,0:T(8,128)(2,1)S(1)} %convolution_convert_fusion.1), kind=kLoop, calls=%fused_computation | loop fusion | flops 8388608 | bytes 33554432 | tf_op jit(solution)/shard_map/concatenate | solution.py:53
  (14 shorter events, 0.3 us)
Async XLA Ops:
  6.5 59.7 %all-gather.4.cloned.1.call-start = ((), (), s32[]{:S(2)}) async-start(), calls=%async_computation.2 | async-start | bytes 9437184 | tf_op jit(solution)/shard_map/all_gather | solution.py:33
  7.3 92.2 %reduce-scatter.3.cloned.1.call-start = ((), (), s32[]{:S(2)}) async-start(), calls=%async_computation.3 | async-start | bytes 1228800 | tf_op jit(solution)/shard_map/reduce_scatter | solution.py:37
  73.0 6.8 %copy-start.2 = (s32[16,1]{0,1:T(1,128)S(1)}, s32[16,1]{0,1:T(1,128)}, u32[]{:S(2)}) copy-start(s32[16,1]{0,1:T(1,128)} %param.9) | copy-start | bytes 196
  73.0 7.0 %copy-start.1 = (bf16[256,120]{0,1:T(8,128)(2,1)S(1)}, bf16[256,120]{0,1:T(8,128)(2,1)}, u32[]{:S(2)}) copy-start(bf16[256,120]{0,1:T(8,128)(2,1)} %param.8) | copy-start | bytes 184324
  73.0 17.9 %copy-start = (bf16[4,120,120]{2,1,0:T(8,128)(2,1)S(1)}, bf16[4,120,120]{2,1,0:T(8,128)(2,1)}, u32[]{:S(2)}) copy-start(bf16[4,120,120]{2,1,0:T(8,128)(2,1)} %param.6) | copy-start | bytes 345604
  73.0 63.6 %reduce-scatter.5.cloned.1.call-start = ((), (), s32[]{:S(2)}) async-start(), calls=%async_computation.4 | async-start | bytes 1228800 | tf_op jit(solution)/shard_map/reduce_scatter | solution.py:37
Sparse Core Ops, SparseCore 0:
  9.2 56.9 all-gather.3
  73.2 26.2 reduce-scatter.2
  101.8 34.8 reduce-scatter.4
